TPU v7x, 256 devices: a whole 4x4x8 slice. The times are simulated.
256 devices in a mesh: cells: 64 (over y, z_lo, x), bands: 4 (over z_hi, core).
Axes of the slice: x: 4, y: 4, z: 8 (z_hi: 2, z_lo: 4; z = z_hi * 4 + z_lo), core: 2. Of those that a mesh axis runs over, the one named last changes fastest.
Arguments:
- waves: bfloat16 [256, 131072], P('bands', 'cells'), may hold values from -6 to 6
- stiffness: float32 [125, 125], replicated, as said below
- cell_scale: float32 [8192], P('cells'), may hold values from 0.5 to 4
- potential: float32 [131072], P('cells'), may hold values from -2 to 2
- connect: int32 [125, 8192], P(None, 'cells'), may hold values from 0 to 3071
- live_cells: int32 [64], P('cells'), may hold values from 16 to 128, as said below
- shared: int32 [64, 2, 512], P('cells'), may hold values from 0 to 2047
- window: float32 [2], replicated, may hold values from 1 to 4
Outputs:
- filtered: float32 [256, 131072], P('bands', 'cells')
- projected: float32 [256, 256], P('cells', 'bands')
Inputs may be any that keep to these rules, and one draw needn't show every extreme that they name: `live_cells`: at least one partition has all 128 slots live. `stiffness`: symmetric positive definite.
All inputs are finite; a program needn't handle non-finite values.
Results may differ from a plain program's by a relative error of at most 0.0037.
Values may be sent and summed in bfloat16 or wider, within the bound.
No kernel may reach another device: no remote copies, remote signals or barrier semaphores. Data moves between devices by JAX's collectives and lax.ppermute only.
A program may use at most 64 MiB of HBM per device.

v0:
```python
import math
import jax
import jax.numpy as jnp
from jax import lax
from jax.sharding import PartitionSpec as P

sigma_one = -0.5
sigma_two = 1.0 / (2.0 / sigma_one - sigma_one)


def with_halo(block, sides, width):
    for axis, dim in sides:
        count = lax.axis_size(axis)
        forward = [(i, i + 1) for i in range(count - 1)]
        backward = [(target, source) for source, target in forward]
        low = lax.ppermute(
            lax.slice_in_dim(block, block.shape[dim] - width, None, axis=dim), axis, forward
        )
        high = lax.ppermute(lax.slice_in_dim(block, 0, width, axis=dim), axis, backward)
        block = jnp.concatenate([low, block, high], axis=dim)
    return block


def local(waves, stiffness, cell_scale, potential, connect, live_cells, shared, window):
    columns, node_dev = waves.shape
    ghost = shared.shape[2]
    capacity = connect.shape[1]
    shared_rows = shared[0]
    live_count = live_cells[0]
    stiff_rounded = stiffness.astype(jnp.bfloat16)
    center = window[0]
    half_width = window[1]
    block_size = math.gcd(capacity, 128)
    block_turns = capacity // block_size
    potential_row = potential[None, :]

    def with_ghosts(owned):
        packed = jnp.concatenate([owned[:, shared_rows[0]], owned[:, shared_rows[1]]], axis=1)
        bordered = with_halo(packed, (("cells", 1),), ghost)
        return jnp.concatenate([bordered[:, :ghost], owned, bordered[:, 3 * ghost :]], axis=1)

    def assemble(totals):
        packed = jnp.concatenate([totals[:, :ghost], totals[:, ghost + node_dev :]], axis=1)
        bordered = with_halo(packed, (("cells", 1),), ghost)
        owned = totals[:, ghost : ghost + node_dev]
        return (
            owned.at[:, shared_rows[0]]
            .add(bordered[:, :ghost])
            .at[:, shared_rows[1]]
            .add(bordered[:, 3 * ghost :])
        )

    def cell_terms(extended):

        def one_block(turn, totals):
            first_cell = turn * block_size
            alive = (first_cell + jnp.arange(block_size) < live_count).astype(jnp.float32)
            weight = cell_scale * alive
            gathered = extended[:, connect]
            product = jnp.einsum(
                "ij,wjb->wib", stiff_rounded, gathered, preferred_element_type=jnp.float32
            )
            return totals.at[:, connect.reshape(-1)].add(
                (product * weight[None, None, :]).reshape(columns, -1)
            )

        empty = jnp.zeros((columns, extended.shape[1]), jnp.float32)
        return lax.fori_loop(0, block_turns, one_block, empty)

    waves32 = waves.astype(jnp.float32)
    applied_x = assemble(cell_terms(with_ghosts(waves))) + potential_row * waves32
    first_pass = ((applied_x - center * waves32) * (sigma_one / half_width)).astype(jnp.bfloat16)
    first32 = first_pass.astype(jnp.float32)
    applied_y = assemble(cell_terms(with_ghosts(first_pass))) + potential_row * first32
    filtered = (applied_y - center * first32) * (
        2.0 * sigma_two / half_width
    ) - sigma_one * sigma_two * waves32
    wave_rounded = filtered.astype(jnp.bfloat16)
    applied = assemble(cell_terms(with_ghosts(wave_rounded))) + potential_row * filtered
    apply_rounded = applied.astype(jnp.bfloat16)
    cell_count = lax.axis_size("cells")
    band_count = lax.axis_size("bands")
    inverse_total = 1.0 / (node_dev * cell_count)
    waves_all = columns * band_count
    own_rows = waves_all // cell_count
    swapped = (
        lax.all_to_all(wave_rounded, "bands", split_axis=1, concat_axis=0, tiled=True),
        lax.all_to_all(apply_rounded, "bands", split_axis=1, concat_axis=0, tiled=True),
    )
    left_side, right_side = swapped
    partial_value = (
        jnp.einsum("wn,vn->wv", left_side, right_side, preferred_element_type=jnp.float32)
        * inverse_total
    )
    arranged = partial_value.reshape(cell_count, own_rows, band_count, columns).transpose(
        0, 2, 1, 3
    )
    arranged = arranged.reshape(cell_count * band_count * own_rows, columns)
    projected = lax.psum_scatter(arranged, ("cells", "bands"), scatter_dimension=0, tiled=True)
    return (filtered, projected)


def solution(mesh):
    return jax.shard_map(
        local,
        mesh=mesh,
        in_specs=(
            P("bands", "cells"),
            P(),
            P("cells"),
            P("cells"),
            P(None, "cells"),
            P("cells"),
            P("cells", None, None),
            P(),
        ),
        out_specs=(P("bands", "cells"), P("cells", "bands")),
        check_vma=False,
    )
```

profile of v0, /device:TPU:2, one launch (start us, length us, event | category | flops | bytes accessed | tf_op | source)
XLA Modules:
  0.0 876.6 jit_solution(12638549431420464733)
XLA Ops:
  22.9 33.0 %gather_fusion.2 = bf16[16000,64]{1,0:T(8,128)(2,1)} fusion(bf16[64,3072]{0,1:T(8,128)(2,1)S(1)} %pad_maximum_fusion, s32[16384]{0:T(1024)S(1)} %pad_clamp_fusion), kind=kCustom, calls=%fused_computation.2 | custom fusion | bytes 4160000 | tf_op jit(solution)/shard_map/while/body/eval_jaxpr/gather | solution.py:59
  55.9 7.4 copy.39
  66.0 5.7 copy.40
  71.6 6.5 copy.63
  78.1 6.8 copy.41
  84.9 88.3 %scatter_custom_fusion = f32[64,3072]{0,1:T(8,128)S(1)} fusion(s32[16000]{0:T(1024)S(1)} %fusion.30, f32[16000,64]{1,0:T(8,128)} %copy.41, f32[]{:T(128)} %constant.22.clone.1), kind=kCustom, calls=%fused_computation.49 | custom fusion | flops 1024000 | bytes 786944 | tf_op jit(solution)/shard_map/while/body/eval_jaxpr/scatter-add | solution.py:63
  206.8 33.0 %gather_fusion.5 = bf16[16000,64]{1,0:T(8,128)(2,1)} fusion(bf16[64,3072]{0,1:T(8,128)(2,1)S(1)} %pad_maximum_fusion.1, s32[16384]{0:T(1024)S(1)} %pad_clamp_fusion), kind=kCustom, calls=%fused_computation.5 | custom fusion | bytes 4160000 | tf_op jit(solution)/shard_map/while/body/eval_jaxpr/gather | solution.py:59
  239.8 7.3 copy.43
  249.8 5.7 copy.44
  255.5 6.5 copy.62
  261.9 6.8 copy.45
  268.7 88.3 %scatter_custom_fusion.3 = f32[64,3072]{0,1:T(8,128)S(1)} fusion(s32[16000]{0:T(1024)} %copy-done.3, f32[16000,64]{1,0:T(8,128)} %copy.45, f32[]{:T(128)} %constant.22.clone.1), kind=kCustom, calls=%fused_computation.47 | custom fusion | flops 1024000 | bytes 786944 | tf_op jit(solution)/shard_map/while/body/eval_jaxpr/scatter-add | solution.py:63
  365.4 5.5 scatter_custom_fusion.4
  371.9 5.3 scatter_custom_fusion.5
  382.1 5.1 collective-permute-start.8
  390.0 7.6 all-to-all-start
  397.8 33.0 %gather_fusion.8 = bf16[16000,64]{1,0:T(8,128)(2,1)} fusion(bf16[64,3072]{0,1:T(8,128)(2,1)S(1)} %pad_maximum_fusion.2, s32[16384]{0:T(1024)S(1)} %pad_clamp_fusion), kind=kCustom, calls=%fused_computation.8 | custom fusion | bytes 4160000 | tf_op jit(solution)/shard_map/while/body/eval_jaxpr/gather | solution.py:59
  430.7 7.9 copy.47
  442.9 5.7 copy.48
  448.6 6.4 copy.61
  455.0 6.8 copy.49
  461.8 89.2 %scatter_custom_fusion.6 = f32[64,3072]{0,1:T(8,128)} fusion(s32[16000]{0:T(1024)} %copy-done.3, f32[16000,64]{1,0:T(8,128)} %copy.49, f32[]{:T(128)} %constant.22.clone.1), kind=kCustom, calls=%fused_computation.45 | custom fusion | flops 1024000 | bytes 786944 | tf_op jit(solution)/shard_map/while/body/eval_jaxpr/scatter-add | solution.py:63
  571.3 19.3 %all_to_all.38 = bf16[64,4,512]{2,0,1:T(8,128)(2,1)S(1)} all-to-all(bf16[64,4,512]{2,0,1:T(8,128)(2,1)S(1)} %copy.50), channel_id=1, replica_groups=mesh['cells'=64,'bands'=4] {'bands'}, dimensions={1} | all-to-all | bytes 524288 | tf_op jit(solution)/shard_map/all_to_all | solution.py:88
  593.2 274.8 %all-reduce.3.cloned.1.call-done = f32[1024,64]{1,0:T(8,128)} async-done(((f32[1024,64]{1,0:T(8,128)}), f32[1024,64]{1,0:T(8,128)}) %all-reduce.3.cloned.1.call-update) | async-done | bytes 262160
  (89 shorter events, 98.1 us)
Async XLA Ops:
  7.2 12.7 %copy-start.1 = (s32[125,128]{1,0:T(8,128)S(1)}, s32[125,128]{1,0:T(8,128)}, u32[]{:S(2)}) copy-start(s32[125,128]{1,0:T(8,128)} %param.12) | copy-start | bytes 192004
  7.2 12.9 %copy-start.10 = (f32[128]{0:T(128)S(1)}, f32[128]{0:T(128)}, u32[]{:S(2)}) copy-start(f32[128]{0:T(128)} %param.10) | copy-start | bytes 1540
  7.2 13.0 %copy-start.9 = (f32[2]{0:T(128)S(1)}, f32[2]{0:T(128)}, u32[]{:S(2)}) copy-start(f32[2]{0:T(128)} %param.15) | copy-start | bytes 28
  8.0 7.9 copy-start.5
  11.1 10.2 %collective-permute-start = (bf16[64,512]{0,1:T(8,128)(2,1)S(1)}, bf16[64,512]{0,1:T(8,128)(2,1)S(1)}, u32[]{:S(2)}, u32[]{:S(2)}) collective-permute-start(bf16[64,512]{0,1:T(8,128)(2,1)S(1)} %bitcast.116), channel_id=1, source_target_pairs={{0,4},{4,8},{8,12},{12,16},{16,20},{20,24},{24,28},{28,32},{32,36}... | collective-permute-start | bytes 196616 | tf_op jit(solution)/shard_map/ppermute | solution.py:16
  15.9 6.9 collective-permute-start.1
  20.1 64.8 %copy-start.3 = (s32[16000]{0:T(1024)}, s32[16000]{0:T(1024)S(1)}, u32[]{:S(2)}) copy-start(s32[16000]{0:T(1024)S(1)} %fusion.30) | copy-start | bytes 192004
  20.1 43.1 %copy-start.6 = (f32[128]{0:T(128)}, f32[128]{0:T(128)S(1)}, u32[]{:S(2)}) copy-start(f32[128]{0:T(128)S(1)} %compare_select_fusion.4) | copy-start | bytes 1540
  55.9 7.4 copy-start
  84.9 95.6 %copy-start.2 = (f32[2048]{0:T(1024)S(1)}, f32[2048]{0:T(1024)}, u32[]{:S(2)}) copy-start(f32[2048]{0:T(1024)} %param.11) | copy-start | bytes 24580
  174.0 8.6 collective-permute-start.2
  177.2 10.6 %collective-permute-start.3 = (f32[64,512]{0,1:T(8,128)}, f32[64,512]{0,1:T(8,128)S(1)}, u32[]{:S(2)}, u32[]{:S(2)}) collective-permute-start(f32[64,512]{0,1:T(8,128)} %get-tuple-element.70), channel_id=1, source_target_pairs={{4,0},{8,4},{12,8},{16,12},{20,16},{24,20},{28,24},{32,28},{36,32}... | collective-permute-start | bytes 393224 | tf_op jit(solution)/shard_map/ppermute | solution.py:19
  195.1 6.9 collective-permute-start.4
  198.8 7.9 collective-permute-start.5
  239.8 7.3 copy-start.7
  357.1 8.3 collective-permute-start.6
  361.6 10.4 %collective-permute-start.7 = (f32[64,512]{0,1:T(8,128)S(1)}, f32[64,512]{0,1:T(8,128)S(1)}, u32[]{:S(2)}, u32[]{:S(2)}) collective-permute-start(f32[64,512]{0,1:T(8,128)S(1)} %get-tuple-element.68), channel_id=1, source_target_pairs={{4,0},{8,4},{12,8},{16,12},{20,16},{24,20},{28,24},{32,28},{36,32}... | collective-permute-start | bytes 393224 | tf_op jit(solution)/shard_map/ppermute | solution.py:19
  382.1 15.5 %collective-permute-start.8 = (bf16[64,512]{0,1:T(8,128)(2,1)S(1)}, bf16[64,512]{0,1:T(8,128)(2,1)S(1)}, u32[]{:S(2)}, u32[]{:S(2)}) collective-permute-start(bf16[64,512]{0,1:T(8,128)(2,1)S(1)} %bitcast.119), channel_id=1, source_target_pairs={{0,4},{4,8},{8,12},{12,16},{16,20},{20,24},{24,28},{28,32},{32,36}... | collective-permute-start | bytes 196616 | tf_op jit(solution)/shard_map/ppermute | solution.py:16
  387.2 10.4 %collective-permute-start.9 = (bf16[64,512]{0,1:T(8,128)(2,1)S(1)}, bf16[64,512]{0,1:T(8,128)(2,1)S(1)}, u32[]{:S(2)}, u32[]{:S(2)}) collective-permute-start(bf16[64,512]{0,1:T(8,128)(2,1)S(1)} %bitcast.117), channel_id=1, source_target_pairs={{4,0},{8,4},{12,8},{16,12},{20,16},{24,20},{28,24},{32,28},{36,32}... | collective-permute-start | bytes 196616 | tf_op jit(solution)/shard_map/ppermute | solution.py:19
  390.0 181.3 %all-to-all-start = ((bf16[64,4,512]{2,0,1:T(8,128)(2,1)}), bf16[64,4,512]{2,0,1:T(8,128)(2,1)S(1)}, u32[]{:S(2)}, u32[]{:S(2)}) async-start(bf16[64,4,512]{2,0,1:T(8,128)(2,1)} %copy.46), calls=%async_computation | async-start | bytes 524288 | tf_op jit(solution)/shard_map/all_to_all | solution.py:87
  397.6 470.4 %all-reduce.3.cloned.1.call-start = ((), (), s32[]{:S(2)}) async-start(), calls=%async_computation.2 | async-start | bytes 1048576
  430.7 7.9 copy-start.8
  552.1 10.6 %collective-permute-start.10 = (f32[64,512]{0,1:T(8,128)S(1)}, f32[64,512]{0,1:T(8,128)S(1)}, u32[]{:S(2)}, u32[]{:S(2)}) collective-permute-start(f32[64,512]{0,1:T(8,128)S(1)} %get-tuple-element.67), channel_id=1, source_target_pairs={{0,4},{4,8},{8,12},{12,16},{16,20},{20,24},{24,28},{28,32},{32,36}... | collective-permute-start | bytes 393224 | tf_op jit(solution)/shard_map/ppermute | solution.py:16
  556.5 10.7 %collective-permute-start.11 = (f32[64,512]{0,1:T(8,128)S(1)}, f32[64,512]{0,1:T(8,128)S(1)}, u32[]{:S(2)}, u32[]{:S(2)}) collective-permute-start(f32[64,512]{0,1:T(8,128)S(1)} %get-tuple-element.66), channel_id=1, source_target_pairs={{4,0},{8,4},{12,8},{16,12},{20,16},{24,20},{28,24},{32,28},{36,32}... | collective-permute-start | bytes 393224 | tf_op jit(solution)/shard_map/ppermute | solution.py:19
  (1 other events, 0.6 us)
Sparse Core Ops, SparseCore 0:
  592.2 275.7 all-reduce.2
where the time goes:
time: 886 us; the launch traced here: 877 us
  other arithmetic  301 us (34%)
  waiting for transfers between devices  289 us (33%)
  local copies, waits for them, and re-layouts  195 us (22%)
  starting transfers between devices  45.7 us (5%)
  blocking collectives  19.3 us (2%)
  between operations  16.8 us (2%)
  matrix products  9.84 us (1%)
    unnamed x2, waiting for transfers between devices  275 us
    scatter-add x3, other arithmetic, one_block(): totals.at[:, connect.reshape(-1)]  266 us
    gather x6, local copies, waits for them, and re-layouts, one_block(): gathered = extended[:, connect]  121 us
    scatter-add x6, other arithmetic, assemble(): return owned.at[:, shared_rows[0]].add(bordered[:, :ghost]).at[:, shared_...  26.6 us
    ppermute x6, starting transfers between devices, with_halo(): lax.ppermute(lax.slice_in_dim(block, block.shape[dim] - width, None, axis...  24.2 us
    unnamed x28, local copies, waits for them, and re-layouts  23.6 us
    reshape x3, local copies, waits for them, and re-layouts, one_block(): (product * weight[None, None, :]).reshape(columns, -1)  20.4 us
    all_to_all x1, blocking collectives, local(): lax.all_to_all(apply_rounded, 'bands', split_axis=1, concat_axis=0, tiled...  19.3 us
  transfers between devices with their start and end apart: 14, of which 10 were waited for; matrix products, arithmetic and copies ran while one was open for 21% of the time, Pallas kernels for 0%

commit v1 on v0

--- a/solution.py
+++ b/solution.py
@@ -85,7 +85,12 @@
     own_rows = waves_all // cell_count
     swapped = (
         lax.all_to_all(wave_rounded, "bands", split_axis=1, concat_axis=0, tiled=True),
-        lax.all_to_all(apply_rounded, "bands", split_axis=1, concat_axis=0, tiled=True),
+        jnp.concatenate(
+            lax.all_to_all(
+                jnp.stack(jnp.split(apply_rounded, lax.axis_size("bands"), axis=1)), "bands", 0, 0
+            ),
+            axis=0,
+        ),
     )
     left_side, right_side = swapped
     partial_value = (

time: 886 us -> 885 us (level)
  transfers between devices with their start and end apart: 14 -> 14, of which waited for: 10 -> 9; matrix products, arithmetic and copies ran while one was open for 21% -> 21% of each run, Pallas kernels for 0% -> 0%
where the time goes in v1:
time: 885 us; the launch traced here: 875 us
  other arithmetic  304 us (34%)
  waiting for transfers between devices  288 us (33%)
  local copies, waits for them, and re-layouts  195 us (22%)
  starting transfers between devices  45.7 us (5%)
  between operations  16.9 us (2%)
  blocking collectives  16.5 us (2%)
  matrix products  9.87 us (1%)
    unnamed x2, waiting for transfers between devices  274 us
    scatter-add x3, other arithmetic, one_block(): totals.at[:, connect.reshape(-1)]  265 us
    gather x6, local copies, waits for them, and re-layouts, one_block(): gathered = extended[:, connect]  122 us
    scatter-add x6, other arithmetic, assemble(): return owned.at[:, shared_rows[0]].add(bordered[:, :ghost]).at[:, shared_...  29.5 us
    ppermute x6, starting transfers between devices, with_halo(): lax.ppermute(lax.slice_in_dim(block, block.shape[dim] - width, None, axis...  24.2 us
    unnamed x28, local copies, waits for them, and re-layouts  23 us
    reshape x3, local copies, waits for them, and re-layouts, one_block(): (product * weight[None, None, :]).reshape(columns, -1)  20.4 us
  transfers between devices with their start and end apart: 14, of which 9 were waited for; matrix products, arithmetic and copies ran while one was open for 21% of the time, Pallas kernels for 0%

profile of v1, /device:TPU:2, one launch (start us, length us, event | category | flops | bytes accessed | tf_op | source)
XLA Modules:
  0.0 875.4 jit_solution(16719890908142331901)
XLA Ops:
  22.4 33.1 %gather_fusion.2 = bf16[16000,64]{1,0:T(8,128)(2,1)} fusion(bf16[64,3072]{0,1:T(8,128)(2,1)S(1)} %pad_maximum_fusion, s32[16384]{0:T(1024)S(1)} %pad_clamp_fusion), kind=kCustom, calls=%fused_computation.2 | custom fusion | bytes 4160000 | tf_op jit(solution)/shard_map/while/body/eval_jaxpr/gather | solution.py:59
  55.5 7.4 copy.39
  65.5 5.7 copy.40
  71.2 6.5 copy.63
  77.7 6.8 copy.41
  84.5 88.3 %scatter_custom_fusion = f32[64,3072]{0,1:T(8,128)S(1)} fusion(s32[16000]{0:T(1024)S(1)} %fusion.30, f32[16000,64]{1,0:T(8,128)} %copy.41, f32[]{:T(128)} %constant.22.clone.1), kind=kCustom, calls=%fused_computation.49 | custom fusion | flops 1024000 | bytes 786944 | tf_op jit(solution)/shard_map/while/body/eval_jaxpr/scatter-add | solution.py:63
  206.4 33.1 %gather_fusion.5 = bf16[16000,64]{1,0:T(8,128)(2,1)} fusion(bf16[64,3072]{0,1:T(8,128)(2,1)S(1)} %pad_maximum_fusion.1, s32[16384]{0:T(1024)S(1)} %pad_clamp_fusion), kind=kCustom, calls=%fused_computation.5 | custom fusion | bytes 4160000 | tf_op jit(solution)/shard_map/while/body/eval_jaxpr/gather | solution.py:59
  239.4 7.3 copy.43
  249.5 5.7 copy.44
  255.2 6.5 copy.62
  261.6 6.8 copy.45
  268.4 88.3 %scatter_custom_fusion.3 = f32[64,3072]{0,1:T(8,128)S(1)} fusion(s32[16000]{0:T(1024)} %copy-done.3, f32[16000,64]{1,0:T(8,128)} %copy.45, f32[]{:T(128)} %constant.22.clone.1), kind=kCustom, calls=%fused_computation.47 | custom fusion | flops 1024000 | bytes 786944 | tf_op jit(solution)/shard_map/while/body/eval_jaxpr/scatter-add | solution.py:63
  365.2 5.5 scatter_custom_fusion.4
  371.7 5.3 scatter_custom_fusion.5
  389.6 7.6 all-to-all-start
  397.4 33.1 %gather_fusion.8 = bf16[16000,64]{1,0:T(8,128)(2,1)} fusion(bf16[64,3072]{0,1:T(8,128)(2,1)S(1)} %pad_maximum_fusion.2, s32[16384]{0:T(1024)S(1)} %pad_clamp_fusion), kind=kCustom, calls=%fused_computation.8 | custom fusion | bytes 4160000 | tf_op jit(solution)/shard_map/while/body/eval_jaxpr/gather | solution.py:59
  430.4 8.0 copy.47
  442.6 5.7 copy.48
  448.3 6.4 copy.61
  454.7 6.8 copy.49
  461.5 88.3 %scatter_custom_fusion.6 = f32[64,3072]{0,1:T(8,128)S(1)} fusion(s32[16000]{0:T(1024)} %copy-done.3, f32[16000,64]{1,0:T(8,128)} %copy.49, f32[]{:T(128)} %constant.22.clone.1), kind=kCustom, calls=%fused_computation.45 | custom fusion | flops 1024000 | bytes 786944 | tf_op jit(solution)/shard_map/while/body/eval_jaxpr/scatter-add | solution.py:63
  566.5 5.3 scatter_custom_fusion.8
  573.6 16.5 %all_to_all.24 = bf16[4,64,512]{2,1,0:T(8,128)(2,1)S(1)} all-to-all(bf16[4,64,512]{2,1,0:T(8,128)(2,1)S(1)} %copy.50), channel_id=1, replica_groups=mesh['cells'=64,'bands'=4] {'bands'}, dimensions={0} | all-to-all | bytes 524288 | tf_op jit(solution)/shard_map/all_to_all | solution.py:89
  592.7 274.2 %all-reduce.3.cloned.1.call-done = f32[1024,64]{1,0:T(8,128)} async-done(((f32[1024,64]{1,0:T(8,128)}), f32[1024,64]{1,0:T(8,128)}) %all-reduce.3.cloned.1.call-update) | async-done | bytes 262160
  (91 shorter events, 100.4 us)
Async XLA Ops:
  7.2 12.2 %copy-start.1 = (s32[125,128]{1,0:T(8,128)S(1)}, s32[125,128]{1,0:T(8,128)}, u32[]{:S(2)}) copy-start(s32[125,128]{1,0:T(8,128)} %param.12) | copy-start | bytes 192004
  7.2 12.4 %copy-start.10 = (f32[128]{0:T(128)S(1)}, f32[128]{0:T(128)}, u32[]{:S(2)}) copy-start(f32[128]{0:T(128)} %param.10) | copy-start | bytes 1540
  7.2 12.4 %copy-start.9 = (f32[2]{0:T(128)S(1)}, f32[2]{0:T(128)}, u32[]{:S(2)}) copy-start(f32[2]{0:T(128)} %param.15) | copy-start | bytes 28
  8.0 7.4 copy-start.4
  8.0 7.4 copy-start.5
  10.6 10.3 %collective-permute-start = (bf16[64,512]{0,1:T(8,128)(2,1)S(1)}, bf16[64,512]{0,1:T(8,128)(2,1)S(1)}, u32[]{:S(2)}, u32[]{:S(2)}) collective-permute-start(bf16[64,512]{0,1:T(8,128)(2,1)S(1)} %bitcast.120), channel_id=1, source_target_pairs={{0,4},{4,8},{8,12},{12,16},{16,20},{20,24},{24,28},{28,32},{32,36}... | collective-permute-start | bytes 196616 | tf_op jit(solution)/shard_map/ppermute | solution.py:16
  15.4 6.9 collective-permute-start.1
  19.6 64.9 %copy-start.3 = (s32[16000]{0:T(1024)}, s32[16000]{0:T(1024)S(1)}, u32[]{:S(2)}) copy-start(s32[16000]{0:T(1024)S(1)} %fusion.30) | copy-start | bytes 192004
  19.6 43.2 %copy-start.6 = (f32[128]{0:T(128)}, f32[128]{0:T(128)S(1)}, u32[]{:S(2)}) copy-start(f32[128]{0:T(128)S(1)} %compare_select_fusion.4) | copy-start | bytes 1540
  55.5 7.4 copy-start
  84.5 95.6 %copy-start.2 = (f32[2048]{0:T(1024)S(1)}, f32[2048]{0:T(1024)}, u32[]{:S(2)}) copy-start(f32[2048]{0:T(1024)} %param.11) | copy-start | bytes 24580
  173.6 8.6 collective-permute-start.2
  176.8 10.6 %collective-permute-start.3 = (f32[64,512]{0,1:T(8,128)}, f32[64,512]{0,1:T(8,128)S(1)}, u32[]{:S(2)}, u32[]{:S(2)}) collective-permute-start(f32[64,512]{0,1:T(8,128)} %get-tuple-element.70), channel_id=1, source_target_pairs={{4,0},{8,4},{12,8},{16,12},{20,16},{24,20},{28,24},{32,28},{36,32}... | collective-permute-start | bytes 393224 | tf_op jit(solution)/shard_map/ppermute | solution.py:19
  194.6 6.9 collective-permute-start.4
  198.3 7.9 collective-permute-start.5
  356.8 8.3 collective-permute-start.6
  361.3 10.4 %collective-permute-start.7 = (f32[64,512]{0,1:T(8,128)S(1)}, f32[64,512]{0,1:T(8,128)S(1)}, u32[]{:S(2)}, u32[]{:S(2)}) collective-permute-start(f32[64,512]{0,1:T(8,128)S(1)} %get-tuple-element.68), channel_id=1, source_target_pairs={{4,0},{8,4},{12,8},{16,12},{20,16},{24,20},{28,24},{32,28},{36,32}... | collective-permute-start | bytes 393224 | tf_op jit(solution)/shard_map/ppermute | solution.py:19
  381.7 15.5 %collective-permute-start.8 = (bf16[64,512]{0,1:T(8,128)(2,1)S(1)}, bf16[64,512]{0,1:T(8,128)(2,1)S(1)}, u32[]{:S(2)}, u32[]{:S(2)}) collective-permute-start(bf16[64,512]{0,1:T(8,128)(2,1)S(1)} %bitcast.123), channel_id=1, source_target_pairs={{0,4},{4,8},{8,12},{12,16},{16,20},{20,24},{24,28},{28,32},{32,36}... | collective-permute-start | bytes 196616 | tf_op jit(solution)/shard_map/ppermute | solution.py:16
  386.8 10.4 %collective-permute-start.9 = (bf16[64,512]{0,1:T(8,128)(2,1)S(1)}, bf16[64,512]{0,1:T(8,128)(2,1)S(1)}, u32[]{:S(2)}, u32[]{:S(2)}) collective-permute-start(bf16[64,512]{0,1:T(8,128)(2,1)S(1)} %bitcast.121), channel_id=1, source_target_pairs={{4,0},{8,4},{12,8},{16,12},{20,16},{24,20},{28,24},{32,28},{36,32}... | collective-permute-start | bytes 196616 | tf_op jit(solution)/shard_map/ppermute | solution.py:19
  389.6 183.9 %all-to-all-start = ((bf16[64,4,512]{2,0,1:T(8,128)(2,1)}), bf16[64,4,512]{2,0,1:T(8,128)(2,1)S(1)}, u32[]{:S(2)}, u32[]{:S(2)}) async-start(bf16[64,4,512]{2,0,1:T(8,128)(2,1)} %copy.46), calls=%async_computation | async-start | bytes 524288 | tf_op jit(solution)/shard_map/all_to_all | solution.py:87
  397.2 469.7 %all-reduce.3.cloned.1.call-start = ((), (), s32[]{:S(2)}) async-start(), calls=%async_computation.2 | async-start | bytes 1048576
  430.4 8.0 copy-start.8
  550.6 10.6 %collective-permute-start.10 = (f32[64,512]{0,1:T(8,128)S(1)}, f32[64,512]{0,1:T(8,128)S(1)}, u32[]{:S(2)}, u32[]{:S(2)}) collective-permute-start(f32[64,512]{0,1:T(8,128)S(1)} %get-tuple-element.67), channel_id=1, source_target_pairs={{0,4},{4,8},{8,12},{12,16},{16,20},{20,24},{24,28},{28,32},{32,36}... | collective-permute-start | bytes 393224 | tf_op jit(solution)/shard_map/ppermute | solution.py:16
  555.0 11.5 %collective-permute-start.11 = (f32[64,512]{0,1:T(8,128)}, f32[64,512]{0,1:T(8,128)S(1)}, u32[]{:S(2)}, u32[]{:S(2)}) collective-permute-start(f32[64,512]{0,1:T(8,128)} %get-tuple-element.66), channel_id=1, source_target_pairs={{4,0},{8,4},{12,8},{16,12},{20,16},{24,20},{28,24},{32,28},{36,32}... | collective-permute-start | bytes 393224 | tf_op jit(solution)/shard_map/ppermute | solution.py:19
  (1 other events, 7.3 us)
Sparse Core Ops, SparseCore 0:
  591.7 275.1 all-reduce.2
